TPU v7x, 128 devices: a whole 4x4x4 slice. The times are simulated.
128 devices in a mesh: req: 8 (over y, core), tok: 16 (over x, z).
Axes of the slice: x: 4, y: 4, z: 4, core: 2. Of those that a mesh axis runs over, the one named last changes fastest.
Arguments:
- layer_input: bfloat16 [16384, 2048], P(('req', 'tok')), may hold values from -12 to 12
- q_in: bfloat16 [16384, 2048], P(('req', 'tok')), may hold values from -10 to 10
- k_in: bfloat16 [16384, 2048], P(('req', 'tok')), may hold values from -10 to 10
- v_in: bfloat16 [16384, 2048], P(('req', 'tok')), may hold values from -6 to 6
- segment_ids: int32 [8, 2048], P('req'), may hold values from 0 to 3, never falling along the last dimension, each value on 1 to 1024 neighbouring positions
- lambda_parts: float32 [4, 128], replicated, may hold values from -0.8 to 0.8
- out_weight: bfloat16 [2048, 2048], replicated, may hold values from -0.125 to 0.125
- ffn_gain: float32 [2048], replicated, may hold values from 0.1 to 1.9
- gate_weight: bfloat16 [2048, 5632], P(None, 'req'), may hold values from -0.125 to 0.125
- up_weight: bfloat16 [2048, 5632], P(None, 'req'), may hold values from -0.125 to 0.125
- down_weight: bfloat16 [5632, 2048], P('req'), may hold values from -0.078125 to 0.078125
- next_gain: float32 [2048], replicated, may hold values from 0.1 to 1.9
- qkv_weight: bfloat16 [2048, 6144], P(None, 'req'), may hold values from -0.125 to 0.125
- page_owner: int32 [8, 256], P('req'), may hold values from 0 to 15, as said below
- page_slot: int32 [8, 256], P('req'), may hold values from 0 to 15, as said below
Outputs:
- layer_output: bfloat16 [16384, 2048], P(('req', 'tok'))
- q_next: bfloat16 [16384, 2048], P(('req', 'tok'))
- page_cache: bfloat16 [2048, 8, 4096], P(('req', 'tok'))
Inputs may be any that keep to these rules, and one draw needn't show every extreme that they name: `segment_ids`: segment numbers never fall along a group; each of the 4 prompts of a group has 1 to 1024 tokens, one exactly 1024. `page_owner`: the 16 pages of each device name every device of its request group as owner exactly once. `page_slot`: within a request group every pair of owner and slot is named by exactly one page.
All inputs are finite; a program needn't handle non-finite values.
Results may differ from a plain program's by a relative error of at most 0.017.
Values may be sent and summed in bfloat16 or wider, within the bound.
A program may use at most 192 MiB of HBM per device.

v0:
```python
import math
import jax
import jax.numpy as jnp
from jax import lax
from jax.sharding import PartitionSpec as P

HEADS = 8
PAGE = 8
NEG_FILL = -1e30
LAMBDA_INIT = 0.2
EPSILON = 1e-05


def rms_rows(values):
    return values * lax.rsqrt(jnp.mean(values * values, axis=-1, keepdims=True) + EPSILON)


def lambda_value(lambda_parts):
    first_term = jnp.exp(jnp.sum(lambda_parts[0] * lambda_parts[1]))
    second_term = jnp.exp(jnp.sum(lambda_parts[2] * lambda_parts[3]))
    return first_term - second_term + LAMBDA_INIT


def body(
    layer_input,
    q_in,
    k_in,
    v_in,
    segment_ids,
    lambda_parts,
    out_weight,
    ffn_gain,
    gate_weight,
    up_weight,
    down_weight,
    next_gain,
    qkv_weight,
    page_owner,
    page_slot,
):
    row_count = q_in.shape[0]
    feat_width = q_in.shape[1]
    head_dim = feat_width // (2 * HEADS)
    peer_count = lax.axis_size("tok")
    tok_place = lax.axis_index("tok")
    seg_row = segment_ids[0]
    first_row = tok_place * row_count
    query_places = first_row + jnp.arange(row_count)
    query_segs = lax.dynamic_slice_in_dim(seg_row, first_row, row_count)
    lambda_mix = lambda_value(lambda_parts)
    score_scale = 1.0 / math.sqrt(head_dim)
    query_split = q_in.reshape(row_count, HEADS, 2, head_dim)
    run_max = jnp.full((HEADS, 2, row_count), NEG_FILL, jnp.float32)
    key_rows = lax.all_gather(k_in, "tok", axis=0, tiled=True)
    value_rows = lax.all_gather(v_in, "tok", axis=0, tiled=True)
    piece_len = key_rows.shape[0]
    key_split = key_rows.reshape(piece_len, HEADS, 2, head_dim)
    value_split = value_rows.reshape(piece_len, HEADS, 2 * head_dim)
    key_places = jnp.arange(piece_len)
    visible = (seg_row[None, :] == query_segs[:, None]) & (
        key_places[None, :] <= query_places[:, None]
    )
    scores = (
        jnp.einsum("qhmd,khmd->hmqk", query_split, key_split, preferred_element_type=jnp.float32)
        * score_scale
    )
    scores = jnp.where(visible, scores, NEG_FILL)
    new_max = jnp.maximum(run_max, jnp.max(scores, axis=-1))
    weights = jnp.where(visible, jnp.exp(scores - new_max[..., None]), 0.0)
    totals = jnp.sum(weights, axis=-1)
    weighted = jnp.einsum(
        "hmqk,khe->hmqe",
        weights.astype(jnp.bfloat16),
        value_split,
        preferred_element_type=jnp.float32,
    )
    run_max, totals, weighted = (new_max, totals, weighted)
    map_outputs = weighted / totals[..., None]
    difference = map_outputs[:, 0] - lambda_mix * map_outputs[:, 1]
    head_outputs = rms_rows(difference) * (1.0 - LAMBDA_INIT)
    attention = (
        jnp.transpose(head_outputs, (1, 0, 2)).reshape(row_count, feat_width).astype(jnp.bfloat16)
    )
    residual_mid = (
        layer_input.astype(jnp.float32)
        + jnp.dot(attention, out_weight, preferred_element_type=jnp.float32)
    ).astype(jnp.bfloat16)
    gathered = lax.all_gather(residual_mid, "req", axis=0, tiled=True)
    normed = (rms_rows(gathered.astype(jnp.float32)) * ffn_gain).astype(jnp.bfloat16)
    gate_proj = jnp.dot(normed, gate_weight, preferred_element_type=jnp.float32)
    up_proj = jnp.dot(normed, up_weight, preferred_element_type=jnp.float32)
    hidden = (jax.nn.silu(gate_proj) * up_proj).astype(jnp.bfloat16)
    ffn_own = lax.psum_scatter(
        jnp.dot(hidden, down_weight, preferred_element_type=jnp.float32).astype(jnp.bfloat16),
        "req",
        scatter_dimension=0,
        tiled=True,
    ).astype(jnp.float32)
    layer_output = (residual_mid.astype(jnp.float32) + ffn_own).astype(jnp.bfloat16)
    next_normed = (rms_rows(layer_output.astype(jnp.float32)) * next_gain).astype(jnp.bfloat16)
    projected_cols = jnp.dot(
        lax.all_gather(next_normed, "req", axis=0, tiled=True),
        qkv_weight,
        preferred_element_type=jnp.float32,
    ).astype(jnp.bfloat16)
    projected = lax.all_to_all(projected_cols, "req", split_axis=0, concat_axis=1, tiled=True)
    q_next = projected[:, :feat_width]
    pages_dev = row_count // PAGE
    per_owner = pages_dev // peer_count
    key_values = projected[:, feat_width:].reshape(pages_dev, PAGE, 2 * feat_width)
    owner_all = page_owner[0].reshape(peer_count, pages_dev)
    slot_all = page_slot[0].reshape(peer_count, pages_dev)
    page_numbers = jnp.arange(pages_dev, dtype=jnp.int32)
    my_owners = lax.dynamic_index_in_dim(owner_all, tok_place, 0, keepdims=False)
    send_order = jnp.argsort(my_owners * pages_dev + page_numbers)
    outgoing = key_values[send_order].reshape(peer_count, per_owner, PAGE, 2 * feat_width)
    incoming = lax.all_to_all(outgoing, "tok", split_axis=0, concat_axis=0, tiled=True)
    rank_keys = jnp.where(
        owner_all == tok_place, page_numbers[None, :], pages_dev + page_numbers[None, :]
    )
    chosen_pages = jnp.argsort(rank_keys, axis=1)[:, :per_owner]
    slot_list = jnp.take_along_axis(slot_all, chosen_pages, axis=1).reshape(pages_dev)
    page_cache = (
        jnp.zeros((pages_dev, PAGE, 2 * feat_width), jnp.bfloat16)
        .at[slot_list]
        .set(incoming.reshape(pages_dev, PAGE, 2 * feat_width))
    )
    return (layer_output, q_next, page_cache)


def solution(mesh):
    in_specs = (
        P(("req", "tok"), None),
        P(("req", "tok"), None),
        P(("req", "tok"), None),
        P(("req", "tok"), None),
        P("req", None),
        P(),
        P(),
        P(),
        P(None, "req"),
        P(None, "req"),
        P("req", None),
        P(),
        P(None, "req"),
        P("req", None),
        P("req", None),
    )
    out_specs = (P(("req", "tok"), None), P(("req", "tok"), None), P(("req", "tok"), None, None))
    return jax.shard_map(body, mesh=mesh, in_specs=in_specs, out_specs=out_specs, check_vma=False)
```

profile of v0, /device:TPU:0, one launch (start us, length us, event | category | flops | bytes accessed | tf_op | source)
XLA Modules:
  0.0 395.1 jit_solution(589856986905657744)
XLA Ops:
  7.2 0.0 copy-start
  7.2 0.0 copy-start.7
  7.2 0.0 all-gather.5.cloned.1.call-start
  7.2 2.2 copy.35
  9.4 0.0 all-gather.5.cloned.1.call-update
  9.5 0.0 all-gather.7.cloned.1.call-start
  9.5 2.0 copy.38
  11.6 0.0 all-gather.7.cloned.1.call-update
  11.6 0.0 all-gather.9.cloned.1.call-start
  11.6 2.2 reshape.96
  13.8 0.0 copy-done.7
  13.8 0.6 multiply_reduce_fusion.1
  15.8 0.4 fusion.24
  16.2 75.5 %all-gather.5.cloned.1.call-done = bf16[2048,2048]{0,1:T(8,128)(2,1)} async-done(((bf16[128,2048]{0,1:T(8,128)(2,1)}), bf16[2048,2048]{0,1:T(8,128)(2,1)}) %all-gather.5.cloned.1.call-update) | async-done | bytes 8388624 | tf_op jit(solution)/shard_map/all_gather | solution.py:54
  91.7 6.6 %fusion = (f32[8,2,128]{2,1,0:T(2,128)S(1)}, f32[8,2,128,2048]{3,2,1,0:T(8,128)S(1)}) fusion(pred[128,2048]{1,0:T(8,128)(4,1)S(1)} %fusion.24, bf16[2048,8,2,128]{0,3,2,1:T(8,128)(2,1)} %bitcast.49, bf16[128,8,2,128]{3,2,1,0:T(2,128)(2,1)} %reshape.96), kind=kOutput, calls=%fused_computation.5 | convolution fusion | flops 1086322688 | bytes 25960448 | tf_op jit(solution)/shard_map/qhmd,khmd->hmqk/dot_general | solution.py:64
  98.4 0.0 copy-start.1
  98.4 5.9 %copy-done.1 = f32[8,2,128,2048]{3,2,1,0:T(8,128)} copy-done((f32[8,2,128,2048]{3,2,1,0:T(8,128)}, f32[8,2,128,2048]{3,2,1,0:T(8,128)S(1)}, u32[]{:S(2)}) %copy-start.1) | copy-done | bytes 16777240
  104.3 5.0 %fusion.1 = f32[8,2,128]{2,1,0:T(2,128)S(1)} fusion(f32[8,2,128,2048]{3,2,1,0:T(8,128)S(1)} %get-tuple-element.12, f32[8,2,128]{2,1,0:T(2,128)S(1)} %broadcast_maximum_fusion, pred[128,2048]{1,0:T(8,128)(4,1)S(1)} %fusion.24), kind=kLoop, calls=%fused_computation.6 | loop fusion | flops 20969472 | bytes 17055744 | tf_op jit(solution)/shard_map/reduce_sum | solution.py:70
  109.3 63.0 %all-gather.7.cloned.1.call-done = bf16[2048,2048]{0,1:T(8,128)(2,1)} async-done(((bf16[128,2048]{0,1:T(8,128)(2,1)}), bf16[2048,2048]{0,1:T(8,128)(2,1)}) %all-gather.7.cloned.1.call-update) | async-done | bytes 8388624 | tf_op jit(solution)/shard_map/all_gather | solution.py:55
  172.3 12.6 %broadcast_divide_fusion = f32[8,2,128,256]{3,2,1,0:T(8,128)S(1)} fusion(f32[8,2,128]{2,1,0:T(2,128)S(1)} %fusion.1, bf16[2048,8,256,1]{0,2,3,1:T(8,128)(2,1)} %bitcast.56, f32[8,2,128,2048]{3,2,1,0:T(8,128)} %copy-done.1, f32[8,2,128]{2,1,0:T(2,128)S(1)} %broadcast_maximum_fusion, pred[128,2048]{1,0:T(8,128)(4,1)S(1)} %fusion.24), kind=kOutput, calls=%fused_computation.37 | convolution fusion | flops 2168979456 | bytes 27541504 | tf_op jit(solution)/shard_map/hmqk,khe->hmqe/dot_general | solution.py:71
  184.9 0.2 multiply_reduce_fusion
  185.1 1.1 fusion.25
  186.2 2.0 copy.40
  188.3 5.7 %fusion.13 = bf16[128,2048]{1,0:T(8,128)(2,1)} fusion(bf16[128,2048]{0,1:T(8,128)(2,1)} %bitcast.53, bf16[2048,2048]{1,0:T(8,128)(2,1)} %param.21, bf16[128,2048]{1,0:T(8,128)(2,1)} %param.15), kind=kOutput, calls=%fused_computation.22 | convolution fusion | flops 1074528256 | bytes 9961472 | tf_op jit(solution)/shard_map/dot_general | solution.py:86
  193.9 0.0 all-gather.9.cloned.1.call-update
  193.9 0.2 reduce-scatter.2.cloned.1.call-start
  194.2 31.3 %all-gather.9.cloned.1.call-done = bf16[1024,2048]{1,0:T(8,128)(2,1)} async-done(((bf16[128,2048]{1,0:T(8,128)(2,1)}), bf16[1024,2048]{1,0:T(8,128)(2,1)}) %all-gather.9.cloned.1.call-update) | async-done | bytes 4194320 | tf_op jit(solution)/shard_map/all_gather | solution.py:88
  225.5 3.2 fusion.3
  228.7 0.0 copy-done.10
  228.7 0.2 copy-done.3
  228.9 6.7 %fusion.15 = f32[1024,704]{0,1:T(8,128)} fusion(bf16[2048,704]{0,1:T(8,128)(2,1)} %param.23, bf16[1024,2048]{1,0:T(8,128)(2,1)S(1)} %copy-done.3, f32[2048]{0:T(1024)S(1)} %copy-done.10, f32[1024]{0:T(1024)S(1)} %add_rsqrt_fusion), kind=kOutput, calls=%fused_computation.26 | convolution fusion | flops 2961178624 | bytes 9973760 | tf_op jit(solution)/shard_map/dot_general | solution.py:90
  235.7 12.4 %convolution_convert_fusion = bf16[1024,2048]{1,0:T(8,128)(2,1)} fusion(bf16[704,2048]{1,0:T(8,128)(2,1)} %param.25, f32[1024,704]{0,1:T(8,128)} %fusion.15, bf16[2048,704]{0,1:T(8,128)(2,1)} %param.24, bf16[1024,2048]{1,0:T(8,128)(2,1)} %all-gather.9.cloned.1.call-done, f32[2048]{0:T(1024)S(1)} %copy-done.10, f32[1024]{0:T(1024)S(1)} %add_rsqrt_fusion), kind=kOutput, calls=%fused_computation.19 | convolution fusion | flops 5920391168 | bytes 17051648 | tf_op jit(solution)/shard_map/dot_general | solution.py:94
  248.1 0.0 reduce-scatter.2.cloned.1.call-update
  248.1 0.0 all-gather.11.cloned.1.call-start
  248.1 37.9 %reduce-scatter.2.cloned.1.call-done = bf16[128,2048]{1,0:T(8,128)(2,1)} async-done(((bf16[1024,2048]{1,0:T(8,128)(2,1)}), bf16[128,2048]{1,0:T(8,128)(2,1)}) %reduce-scatter.2.cloned.1.call-update) | async-done | bytes 524304 | tf_op jit(solution)/shard_map/reduce_scatter | solution.py:93
  286.0 1.5 fusion.19
  287.5 0.8 copy-done.4
  288.3 1.0 fusion.21
  289.2 0.0 all-gather.11.cloned.1.call-update
  289.3 0.0 copy-start.8
  289.3 0.0 copy-start.9
  289.3 31.2 %all-gather.11.cloned.1.call-done = bf16[1024,2048]{1,0:T(8,128)(2,1)} async-done(((bf16[128,2048]{1,0:T(8,128)(2,1)}), bf16[1024,2048]{1,0:T(8,128)(2,1)}) %all-gather.11.cloned.1.call-update) | async-done | bytes 4194320 | tf_op jit(solution)/shard_map/all_gather | solution.py:102
  320.4 6.8 %convolution_convert_fusion.1 = bf16[1024,768]{1,0:T(8,128)(2,1)} fusion(bf16[1024,2048]{1,0:T(8,128)(2,1)} %all-gather.11.cloned.1.call-done, bf16[2048,768]{1,0:T(8,128)(2,1)S(1)} %copy-done), kind=kOutput, calls=%fused_computation.23 | convolution fusion | flops 3222011904 | bytes 8912896 | tf_op jit(solution)/shard_map/dot_general | solution.py:101
  327.2 4.3 %all-to-all-start = ((bf16[8,128,768]{2,1,0:T(8,128)(2,1)}), bf16[8,128,768]{2,1,0:T(8,128)(2,1)}, u32[]{:S(2)}, u32[]{:S(2)}) async-start(bf16[8,128,768]{2,1,0:T(8,128)(2,1)} %bitcast.54), calls=%async_computation.1 | async-start | bytes 3145728 | tf_op jit(solution)/shard_map/all_to_all | solution.py:106
  331.5 0.5 broadcast.117
  332.0 0.7 reduce.9
  332.7 0.1 reshape_squeeze.6
  332.8 0.1 copy.42
  332.9 0.7 reduce.8
  333.5 0.1 reshape_squeeze.7
  333.6 1.2 sort.35
  334.9 18.2 %all-to-all-done = bf16[8,128,768]{2,1,0:T(8,128)(2,1)} async-done(((bf16[8,128,768]{2,1,0:T(8,128)(2,1)}), bf16[8,128,768]{2,1,0:T(8,128)(2,1)}, u32[]{:S(2)}, u32[]{:S(2)}) %all-to-all-start) | async-done | bytes 1572896 | tf_op jit(solution)/shard_map/all_to_all | solution.py:106
  353.1 1.6 copy.47
  354.7 1.1 copy-done.2
  355.8 1.0 slice_bitcast_fusion
  356.9 2.8 gather_fusion
  359.7 7.0 %all-to-all-start.1 = ((bf16[16,1,8,4096]{3,2,1,0:T(8,128)(2,1)}), bf16[16,1,8,4096]{3,2,1,0:T(8,128)(2,1)}, u32[]{:S(2)}, u32[]{:S(2)}) async-start(bf16[16,1,8,4096]{3,2,1,0:T(8,128)(2,1)} %bitcast.52), calls=%async_computation.2 | async-start | bytes 2097152 | tf_op jit(solution)/shard_map/all_to_all | solution.py:117
  366.7 0.1 iota_select_fusion
  366.8 0.7 sort.34
  367.5 0.7 gather_fusion.1
  368.2 1.9 slice.42
  370.1 14.1 %all-to-all-done.1 = bf16[16,1,8,4096]{3,2,1,0:T(8,128)(2,1)} async-done(((bf16[16,1,8,4096]{3,2,1,0:T(8,128)(2,1)}), bf16[16,1,8,4096]{3,2,1,0:T(8,128)(2,1)}, u32[]{:S(2)}, u32[]{:S(2)}) %all-to-all-start.1) | async-done | bytes 1048608 | tf_op jit(solution)/shard_map/all_to_all | solution.py:117
  384.1 1.1 broadcast_in_dim.54
  385.2 3.4 scatter_fusion
  (28 shorter events, 0.1 us)
Async XLA Ops:
  7.2 313.3 %copy-start = (bf16[2048,768]{1,0:T(8,128)(2,1)S(1)}, bf16[2048,768]{1,0:T(8,128)(2,1)}, u32[]{:S(2)}) copy-start(bf16[2048,768]{1,0:T(8,128)(2,1)} %param.27) | copy-start | bytes 9437188
  7.2 6.7 %copy-start.7 = (f32[4,128]{1,0:T(4,128)S(1)}, f32[4,128]{1,0:T(4,128)}, u32[]{:S(2)}) copy-start(f32[4,128]{1,0:T(4,128)} %param.20) | copy-start | bytes 6148
  7.2 8.6 %copy-start.6 = (s32[1,2048]{1,0:T(1,128)S(1)}, s32[1,2048]{1,0:T(1,128)}, u32[]{:S(2)}) copy-start(s32[1,2048]{1,0:T(1,128)} %param.19) | copy-start | bytes 24580
  7.2 84.5 %all-gather.5.cloned.1.call-start = ((), (), s32[]{:S(2)}) async-start(), calls=%async_computation.3 | async-start | bytes 8912896 | tf_op jit(solution)/shard_map/all_gather | solution.py:54
  9.5 162.8 %all-gather.7.cloned.1.call-start = ((), (), s32[]{:S(2)}) async-start(), calls=%async_computation.4 | async-start | bytes 8912896 | tf_op jit(solution)/shard_map/all_gather | solution.py:55
  11.6 213.9 %all-gather.9.cloned.1.call-start = ((), (), s32[]{:S(2)}) async-start(), calls=%async_computation.5 | async-start | bytes 4718592 | tf_op jit(solution)/shard_map/all_gather | solution.py:88
  98.4 5.9 %copy-start.1 = (f32[8,2,128,2048]{3,2,1,0:T(8,128)}, f32[8,2,128,2048]{3,2,1,0:T(8,128)S(1)}, u32[]{:S(2)}) copy-start(f32[8,2,128,2048]{3,2,1,0:T(8,128)S(1)} %get-tuple-element.12) | copy-start | bytes 50331652
  193.9 34.8 %copy-start.10 = (f32[2048]{0:T(1024)S(1)}, f32[2048]{0:T(1024)}, u32[]{:S(2)}) copy-start(f32[2048]{0:T(1024)} %param.22) | copy-start | bytes 24580
  193.9 92.0 %reduce-scatter.2.cloned.1.call-start = ((), (), s32[]{:S(2)}) async-start(), calls=%async_computation.6 | async-start | bytes 4718592 | tf_op jit(solution)/shard_map/reduce_scatter | solution.py:93
  225.5 3.4 copy-start.3
  248.1 40.2 %copy-start.5 = (f32[2048]{0:T(1024)S(1)}, f32[2048]{0:T(1024)}, u32[]{:S(2)}) copy-start(f32[2048]{0:T(1024)} %param.26) | copy-start | bytes 24580
  248.1 72.4 %all-gather.11.cloned.1.call-start = ((), (), s32[]{:S(2)}) async-start(), calls=%async_computation.7 | async-start | bytes 4718592 | tf_op jit(solution)/shard_map/all_gather | solution.py:102
  287.5 0.8 copy-start.4
  289.3 42.8 %copy-start.8 = (s32[1,256]{1,0:T(1,128)S(1)}, s32[1,256]{1,0:T(1,128)}, u32[]{:S(2)}) copy-start(s32[1,256]{1,0:T(1,128)} %param.28) | copy-start | bytes 3076
  289.3 43.6 %copy-start.9 = (s32[1,256]{1,0:T(1,128)S(1)}, s32[1,256]{1,0:T(1,128)}, u32[]{:S(2)}) copy-start(s32[1,256]{1,0:T(1,128)} %param.29) | copy-start | bytes 3076
  327.2 25.9 %all-to-all-start = ((bf16[8,128,768]{2,1,0:T(8,128)(2,1)}), bf16[8,128,768]{2,1,0:T(8,128)(2,1)}, u32[]{:S(2)}, u32[]{:S(2)}) async-start(bf16[8,128,768]{2,1,0:T(8,128)(2,1)} %bitcast.54), calls=%async_computation.1 | async-start | bytes 3145728 | tf_op jit(solution)/shard_map/all_to_all | solution.py:106
  354.7 1.2 copy-start.2
  359.7 24.4 %all-to-all-start.1 = ((bf16[16,1,8,4096]{3,2,1,0:T(8,128)(2,1)}), bf16[16,1,8,4096]{3,2,1,0:T(8,128)(2,1)}, u32[]{:S(2)}, u32[]{:S(2)}) async-start(bf16[16,1,8,4096]{3,2,1,0:T(8,128)(2,1)} %bitcast.52), calls=%async_computation.2 | async-start | bytes 2097152 | tf_op jit(solution)/shard_map/all_to_all | solution.py:117
Sparse Core Ops, SparseCore 0:
  10.7 80.9 all-gather.4
  94.4 77.8 all-gather.6
  194.1 31.3 all-gather.8
  248.2 37.7 reduce-scatter.1
  289.4 31.0 all-gather.10
where the time goes:
time: 396 us; the launch traced here: 395 us
  waiting for transfers between devices  271 us (68%)
  matrix products  50.8 us (13%)
  local copies, waits for them, and re-layouts  29.8 us (8%)
  other arithmetic  16.5 us (4%)
  between operations  15.3 us (4%)
  starting transfers between devices  11.7 us (3%)
    all_gather x1, waiting for transfers between devices, body(): key_rows = lax.all_gather(k_in, 'tok', axis=0, tiled=True)  75.5 us
    all_gather x1, waiting for transfers between devices, body(): value_rows = lax.all_gather(v_in, 'tok', axis=0, tiled=True)  63 us
    reduce_scatter x1, waiting for transfers between devices, body(): lax.psum_scatter(jnp.dot(hidden, down_weight, preferred_element_type=jnp....  37.9 us
    all_gather x1, waiting for transfers between devices, body(): gathered = lax.all_gather(residual_mid, 'req', axis=0, tiled=True)  31.3 us
    all_gather x1, waiting for transfers between devices, body(): lax.all_gather(next_normed, 'req', axis=0, tiled=True)  31.2 us
    all_to_all x1, waiting for transfers between devices, body(): lax.all_to_all(projected_cols, 'req', split_axis=0, concat_axis=1, tiled=...  18.2 us
    all_to_all x1, waiting for transfers between devices, body(): lax.all_to_all(outgoing, 'tok', split_axis=0, concat_axis=0, tiled=True)  14.1 us
    unnamed x26, local copies, waits for them, and re-layouts  12.8 us
  transfers between devices with their start and end apart: 7, of which 7 were waited for; matrix products, arithmetic and copies ran while one was open for 6% of the time, Pallas kernels for 0%

commit v1 on v0

--- a/solution.py
+++ b/solution.py
@@ -9,6 +9,13 @@
 NEG_FILL = -1e30
 LAMBDA_INIT = 0.2
 EPSILON = 1e-05
+
+
+def islands_solve(w_in):
+    e_next = lax.axis_size("req")
+    all_rows = jnp.split(w_in, e_next, axis=0)
+    r2 = jnp.stack(all_rows)
+    return jnp.concatenate(lax.all_to_all(r2, "req", 0, 0), axis=1)
 
 
 def rms_rows(values):
@@ -103,7 +110,7 @@
         qkv_weight,
         preferred_element_type=jnp.float32,
     ).astype(jnp.bfloat16)
-    projected = lax.all_to_all(projected_cols, "req", split_axis=0, concat_axis=1, tiled=True)
+    projected = islands_solve(projected_cols)
     q_next = projected[:, :feat_width]
     pages_dev = row_count // PAGE
     per_owner = pages_dev // peer_count

time: 396 us -> 404 us (1.020)
  local copies, waits for them, and re-layouts: 29.8 us -> 40.6 us
    unnamed x26 -> x32, local copies, waits for them, and re-layouts: 12.8 us -> 18.5 us
    slice x0 -> x2, local copies, waits for them, and re-layouts: none -> 4.52 us  [body(): projected[:, feat_width:].reshape(pages_dev, PAGE, 2 * feat_width)]
where the time goes in v1:
time: 404 us; the launch traced here: 403 us
  waiting for transfers between devices  269 us (67%)
  matrix products  49.6 us (12%)
  local copies, waits for them, and re-layouts  40.6 us (10%)
  other arithmetic  16.5 us (4%)
  between operations  15.3 us (4%)
  starting transfers between devices  11.7 us (3%)
    all_gather x1, waiting for transfers between devices, body(): key_rows = lax.all_gather(k_in, 'tok', axis=0, tiled=True)  75.5 us
    all_gather x1, waiting for transfers between devices, body(): value_rows = lax.all_gather(v_in, 'tok', axis=0, tiled=True)  63 us
    reduce_scatter x1, waiting for transfers between devices, body(): lax.psum_scatter(jnp.dot(hidden, down_weight, preferred_element_type=jnp....  37.9 us
    all_gather x1, waiting for transfers between devices, body(): gathered = lax.all_gather(residual_mid, 'req', axis=0, tiled=True)  31.3 us
    all_gather x1, waiting for transfers between devices, body(): lax.all_gather(next_normed, 'req', axis=0, tiled=True)  31.2 us
    unnamed x32, local copies, waits for them, and re-layouts  18.5 us
    all_to_all x1, waiting for transfers between devices, islands_solve(): return jnp.concatenate(lax.all_to_all(r2, 'req', 0, 0), axis=1)  18.2 us
    dot_general x1, matrix products, body(): jnp.einsum('hmqk,khe->hmqe', weights.astype(jnp.bfloat16), value_split, p...  12.6 us
  transfers between devices with their start and end apart: 7, of which 7 were waited for; matrix products, arithmetic and copies ran while one was open for 6% of the time, Pallas kernels for 0%

profile of v1, /device:TPU:0, one launch (start us, length us, event | category | flops | bytes accessed | tf_op | source)
XLA Modules:
  0.0 402.8 jit_solution(12794447956444543740)
XLA Ops:
  7.2 0.0 all-gather.5.cloned.1.call-start
  7.2 2.2 copy.37
  9.4 0.0 all-gather.5.cloned.1.call-update
  9.5 0.0 all-gather.7.cloned.1.call-start
  9.5 2.0 copy.40
  11.6 0.0 all-gather.7.cloned.1.call-update
  11.6 0.0 all-gather.9.cloned.1.call-start
  11.6 2.2 reshape.99
  13.8 0.6 multiply_reduce_fusion.1
  15.8 0.4 fusion.24
  16.2 75.5 %all-gather.5.cloned.1.call-done = bf16[2048,2048]{0,1:T(8,128)(2,1)} async-done(((bf16[128,2048]{0,1:T(8,128)(2,1)}), bf16[2048,2048]{0,1:T(8,128)(2,1)}) %all-gather.5.cloned.1.call-update) | async-done | bytes 8388624 | tf_op jit(solution)/shard_map/all_gather | solution.py:61
  91.7 6.6 %fusion = (f32[8,2,128]{2,1,0:T(2,128)S(1)}, f32[8,2,128,2048]{3,2,1,0:T(8,128)S(1)}) fusion(pred[128,2048]{1,0:T(8,128)(4,1)S(1)} %fusion.24, bf16[2048,8,2,128]{0,3,2,1:T(8,128)(2,1)} %bitcast.80, bf16[128,8,2,128]{3,2,1,0:T(2,128)(2,1)} %reshape.99), kind=kOutput, calls=%fused_computation.5 | convolution fusion | flops 1086322688 | bytes 25960448 | tf_op jit(solution)/shard_map/qhmd,khmd->hmqk/dot_general | solution.py:71
  98.4 5.9 %copy-done.1 = f32[8,2,128,2048]{3,2,1,0:T(8,128)} copy-done((f32[8,2,128,2048]{3,2,1,0:T(8,128)}, f32[8,2,128,2048]{3,2,1,0:T(8,128)S(1)}, u32[]{:S(2)}) %copy-start.1) | copy-done | bytes 16777240
  104.3 5.0 %fusion.1 = f32[8,2,128]{2,1,0:T(2,128)S(1)} fusion(f32[8,2,128,2048]{3,2,1,0:T(8,128)S(1)} %get-tuple-element.21, f32[8,2,128]{2,1,0:T(2,128)S(1)} %broadcast_maximum_fusion, pred[128,2048]{1,0:T(8,128)(4,1)S(1)} %fusion.24), kind=kLoop, calls=%fused_computation.6 | loop fusion | flops 20969472 | bytes 17055744 | tf_op jit(solution)/shard_map/reduce_sum | solution.py:77
  109.3 63.0 %all-gather.7.cloned.1.call-done = bf16[2048,2048]{0,1:T(8,128)(2,1)} async-done(((bf16[128,2048]{0,1:T(8,128)(2,1)}), bf16[2048,2048]{0,1:T(8,128)(2,1)}) %all-gather.7.cloned.1.call-update) | async-done | bytes 8388624 | tf_op jit(solution)/shard_map/all_gather | solution.py:62
  172.3 12.6 %broadcast_divide_fusion = f32[8,2,128,256]{3,2,1,0:T(8,128)S(1)} fusion(f32[8,2,128]{2,1,0:T(2,128)S(1)} %fusion.1, bf16[2048,8,256,1]{0,2,3,1:T(8,128)(2,1)} %bitcast.87, f32[8,2,128,2048]{3,2,1,0:T(8,128)} %copy-done.1, f32[8,2,128]{2,1,0:T(2,128)S(1)} %broadcast_maximum_fusion, pred[128,2048]{1,0:T(8,128)(4,1)S(1)} %fusion.24), kind=kOutput, calls=%fused_computation.36 | convolution fusion | flops 2168979456 | bytes 27541504 | tf_op jit(solution)/shard_map/hmqk,khe->hmqe/dot_general | solution.py:78
  184.9 0.2 multiply_reduce_fusion
  185.1 1.1 fusion.25
  186.2 2.0 copy.42
  188.3 5.7 %fusion.13 = bf16[128,2048]{1,0:T(8,128)(2,1)} fusion(bf16[128,2048]{0,1:T(8,128)(2,1)} %bitcast.85, bf16[2048,2048]{1,0:T(8,128)(2,1)} %param.21, bf16[128,2048]{1,0:T(8,128)(2,1)} %param.15), kind=kOutput, calls=%fused_computation.22 | convolution fusion | flops 1074528256 | bytes 9961472 | tf_op jit(solution)/shard_map/dot_general | solution.py:93
  193.9 0.0 all-gather.9.cloned.1.call-update
  193.9 0.2 reduce-scatter.2.cloned.1.call-start
  194.2 31.3 %all-gather.9.cloned.1.call-done = bf16[1024,2048]{1,0:T(8,128)(2,1)} async-done(((bf16[128,2048]{1,0:T(8,128)(2,1)}), bf16[1024,2048]{1,0:T(8,128)(2,1)}) %all-gather.9.cloned.1.call-update) | async-done | bytes 4194320 | tf_op jit(solution)/shard_map/all_gather | solution.py:95
  225.5 3.2 fusion.3
  228.7 0.2 copy-done.2
  228.9 6.7 %fusion.15 = f32[1024,704]{0,1:T(8,128)} fusion(bf16[2048,704]{0,1:T(8,128)(2,1)} %param.23, bf16[1024,2048]{1,0:T(8,128)(2,1)S(1)} %copy-done.2, f32[2048]{0:T(1024)S(1)} %copy-done.9, f32[1024]{0:T(1024)S(1)} %add_rsqrt_fusion), kind=kOutput, calls=%fused_computation.26 | convolution fusion | flops 2961178624 | bytes 9973760 | tf_op jit(solution)/shard_map/dot_general | solution.py:97
  235.7 12.4 %convolution_convert_fusion = bf16[1024,2048]{1,0:T(8,128)(2,1)} fusion(bf16[704,2048]{1,0:T(8,128)(2,1)} %param.25, f32[1024,704]{0,1:T(8,128)} %fusion.15, bf16[2048,704]{0,1:T(8,128)(2,1)} %param.24, bf16[1024,2048]{1,0:T(8,128)(2,1)} %all-gather.9.cloned.1.call-done, f32[2048]{0:T(1024)S(1)} %copy-done.9, f32[1024]{0:T(1024)S(1)} %add_rsqrt_fusion), kind=kOutput, calls=%fused_computation.19 | convolution fusion | flops 5920391168 | bytes 17051648 | tf_op jit(solution)/shard_map/dot_general | solution.py:101
  248.1 0.0 all-gather.11.cloned.1.call-start
  248.1 37.9 %reduce-scatter.2.cloned.1.call-done = bf16[128,2048]{1,0:T(8,128)(2,1)} async-done(((bf16[1024,2048]{1,0:T(8,128)(2,1)}), bf16[128,2048]{1,0:T(8,128)(2,1)}) %reduce-scatter.2.cloned.1.call-update) | async-done | bytes 524304 | tf_op jit(solution)/shard_map/reduce_scatter | solution.py:100
  286.0 1.5 fusion.19
  287.5 0.8 copy-done.3
  288.3 1.0 fusion.21
  289.3 31.2 %all-gather.11.cloned.1.call-done = bf16[1024,2048]{1,0:T(8,128)(2,1)} async-done(((bf16[128,2048]{1,0:T(8,128)(2,1)}), bf16[1024,2048]{1,0:T(8,128)(2,1)}) %all-gather.11.cloned.1.call-update) | async-done | bytes 4194320 | tf_op jit(solution)/shard_map/all_gather | solution.py:109
  320.4 5.6 %convolution_convert_fusion.1 = bf16[1024,768]{1,0:T(8,128)(2,1)S(1)} fusion(bf16[1024,2048]{1,0:T(8,128)(2,1)} %all-gather.11.cloned.1.call-done, bf16[2048,768]{1,0:T(8,128)(2,1)S(1)} %copy-done), kind=kOutput, calls=%fused_computation.23 | convolution fusion | flops 3222011904 | bytes 8912896 | tf_op jit(solution)/shard_map/dot_general | solution.py:108
  326.1 0.7 fusion.35
  326.8 0.7 fusion.34
  327.4 0.7 fusion.33
  328.1 0.7 fusion.32
  328.8 0.7 fusion.31
  329.5 0.7 fusion.30
  330.2 0.7 fusion.29
  330.9 0.7 fusion.28
  331.6 4.3 %all-to-all-start = ((bf16[8,128,768]{2,1,0:T(8,128)(2,1)}), bf16[8,128,768]{2,1,0:T(8,128)(2,1)}, u32[]{:S(2)}, u32[]{:S(2)}) async-start(bf16[8,128,768]{2,1,0:T(8,128)(2,1)} %fusion.28), calls=%async_computation.1 | async-start | bytes 3145728 | tf_op jit(solution)/shard_map/all_to_all | solution.py:18
  335.9 0.5 broadcast.117
  336.4 0.7 reduce.9
  337.1 0.1 reshape_squeeze.6
  337.1 0.1 copy.44
  337.2 0.7 reduce.8
  337.9 0.1 reshape_squeeze.7
  338.0 1.2 sort.35
  339.2 18.2 %all-to-all-done = bf16[8,128,768]{2,1,0:T(8,128)(2,1)} async-done(((bf16[8,128,768]{2,1,0:T(8,128)(2,1)}), bf16[8,128,768]{2,1,0:T(8,128)(2,1)}, u32[]{:S(2)}, u32[]{:S(2)}) %all-to-all-start) | async-done | bytes 1572896 | tf_op jit(solution)/shard_map/all_to_all | solution.py:18
  357.5 2.6 copy.43
  360.1 2.3 slice.43
  362.3 2.3 copy.45
  364.6 2.8 gather_fusion
  367.4 7.0 %all-to-all-start.1 = ((bf16[16,1,8,4096]{3,2,1,0:T(8,128)(2,1)}), bf16[16,1,8,4096]{3,2,1,0:T(8,128)(2,1)}, u32[]{:S(2)}, u32[]{:S(2)}) async-start(bf16[16,1,8,4096]{3,2,1,0:T(8,128)(2,1)} %bitcast.83), calls=%async_computation.2 | async-start | bytes 2097152 | tf_op jit(solution)/shard_map/all_to_all | solution.py:124
  374.4 0.1 iota_select_fusion
  374.5 0.7 sort.34
  375.2 0.7 gather_fusion.1
  375.9 1.9 slice.42
  377.8 2.0 copy.47
  379.8 12.0 %all-to-all-done.1 = bf16[16,1,8,4096]{3,2,1,0:T(8,128)(2,1)} async-done(((bf16[16,1,8,4096]{3,2,1,0:T(8,128)(2,1)}), bf16[16,1,8,4096]{3,2,1,0:T(8,128)(2,1)}, u32[]{:S(2)}, u32[]{:S(2)}) %all-to-all-start.1) | async-done | bytes 1048608 | tf_op jit(solution)/shard_map/all_to_all | solution.py:124
  391.8 1.1 broadcast_in_dim.54
  392.9 3.4 scatter_fusion
  (36 shorter events, 0.2 us)
Async XLA Ops:
  7.2 313.3 %copy-start = (bf16[2048,768]{1,0:T(8,128)(2,1)S(1)}, bf16[2048,768]{1,0:T(8,128)(2,1)}, u32[]{:S(2)}) copy-start(bf16[2048,768]{1,0:T(8,128)(2,1)} %param.27) | copy-start | bytes 9437188
  7.2 6.7 %copy-start.6 = (f32[4,128]{1,0:T(4,128)S(1)}, f32[4,128]{1,0:T(4,128)}, u32[]{:S(2)}) copy-start(f32[4,128]{1,0:T(4,128)} %param.20) | copy-start | bytes 6148
  7.2 8.6 %copy-start.5 = (s32[1,2048]{1,0:T(1,128)S(1)}, s32[1,2048]{1,0:T(1,128)}, u32[]{:S(2)}) copy-start(s32[1,2048]{1,0:T(1,128)} %param.19) | copy-start | bytes 24580
  7.2 84.5 %all-gather.5.cloned.1.call-start = ((), (), s32[]{:S(2)}) async-start(), calls=%async_computation.3 | async-start | bytes 8912896 | tf_op jit(solution)/shard_map/all_gather | solution.py:61
  9.5 162.8 %all-gather.7.cloned.1.call-start = ((), (), s32[]{:S(2)}) async-start(), calls=%async_computation.4 | async-start | bytes 8912896 | tf_op jit(solution)/shard_map/all_gather | solution.py:62
  11.6 213.9 %all-gather.9.cloned.1.call-start = ((), (), s32[]{:S(2)}) async-start(), calls=%async_computation.5 | async-start | bytes 4718592 | tf_op jit(solution)/shard_map/all_gather | solution.py:95
  98.4 5.9 %copy-start.1 = (f32[8,2,128,2048]{3,2,1,0:T(8,128)}, f32[8,2,128,2048]{3,2,1,0:T(8,128)S(1)}, u32[]{:S(2)}) copy-start(f32[8,2,128,2048]{3,2,1,0:T(8,128)S(1)} %get-tuple-element.21) | copy-start | bytes 50331652
  193.9 34.8 %copy-start.9 = (f32[2048]{0:T(1024)S(1)}, f32[2048]{0:T(1024)}, u32[]{:S(2)}) copy-start(f32[2048]{0:T(1024)} %param.22) | copy-start | bytes 24580
  193.9 92.0 %reduce-scatter.2.cloned.1.call-start = ((), (), s32[]{:S(2)}) async-start(), calls=%async_computation.6 | async-start | bytes 4718592 | tf_op jit(solution)/shard_map/reduce_scatter | solution.py:100
  225.5 3.4 copy-start.2
  248.1 40.2 %copy-start.4 = (f32[2048]{0:T(1024)S(1)}, f32[2048]{0:T(1024)}, u32[]{:S(2)}) copy-start(f32[2048]{0:T(1024)} %param.26) | copy-start | bytes 24580
  248.1 72.4 %all-gather.11.cloned.1.call-start = ((), (), s32[]{:S(2)}) async-start(), calls=%async_computation.7 | async-start | bytes 4718592 | tf_op jit(solution)/shard_map/all_gather | solution.py:109
  287.5 0.8 copy-start.3
  326.0 10.3 %copy-start.7 = (s32[1,256]{1,0:T(1,128)S(1)}, s32[1,256]{1,0:T(1,128)}, u32[]{:S(2)}) copy-start(s32[1,256]{1,0:T(1,128)} %param.28) | copy-start | bytes 3076
  326.1 11.2 %copy-start.8 = (s32[1,256]{1,0:T(1,128)S(1)}, s32[1,256]{1,0:T(1,128)}, u32[]{:S(2)}) copy-start(s32[1,256]{1,0:T(1,128)} %param.29) | copy-start | bytes 3076
  331.6 25.9 %all-to-all-start = ((bf16[8,128,768]{2,1,0:T(8,128)(2,1)}), bf16[8,128,768]{2,1,0:T(8,128)(2,1)}, u32[]{:S(2)}, u32[]{:S(2)}) async-start(bf16[8,128,768]{2,1,0:T(8,128)(2,1)} %fusion.28), calls=%async_computation.1 | async-start | bytes 3145728 | tf_op jit(solution)/shard_map/all_to_all | solution.py:18
  367.4 24.4 %all-to-all-start.1 = ((bf16[16,1,8,4096]{3,2,1,0:T(8,128)(2,1)}), bf16[16,1,8,4096]{3,2,1,0:T(8,128)(2,1)}, u32[]{:S(2)}, u32[]{:S(2)}) async-start(bf16[16,1,8,4096]{3,2,1,0:T(8,128)(2,1)} %bitcast.83), calls=%async_computation.2 | async-start | bytes 2097152 | tf_op jit(solution)/shard_map/all_to_all | solution.py:124
Sparse Core Ops, SparseCore 0:
  10.7 80.9 all-gather.4
  94.4 77.8 all-gather.6
  194.1 31.3 all-gather.8
  248.2 37.7 reduce-scatter.1
  289.4 31.0 all-gather.10
